TPU v7x, 512 devices: a whole 4x4x16 slice. The times are simulated.
512 devices in a mesh: req: 128 (over x, z, core), tp: 4 (over y).
Axes of the slice: x: 4, y: 4, z: 16, core: 2. Of those that a mesh axis runs over, the one named last changes fastest.
Arguments:
- x_pre: bfloat16 [65536, 1280], P('req', 'tp'), may hold values from -6 to 6
- x_dec: bfloat16 [512, 1280], P('req', 'tp'), may hold values from -6 to 6
- norm_gain: float32 [1280], replicated, may hold values from 0.1 to 1.9
- w_qkv: bfloat16 [3, 1280, 1280], P(None, None, 'tp'), may hold values from -0.15625 to 0.15625
- w_out: bfloat16 [1280, 1280], P('tp'), may hold values from -0.625 to 0.625
- pre_keys: bfloat16 [49152, 1280], P('req', 'tp'), may hold values from -70 to 70
- pre_values: bfloat16 [49152, 1280], P('req', 'tp'), may hold values from -6 to 6
- pre_lens: int32 [128], P('req'), may hold values from 0 to 384, as said below
- dec_keys: bfloat16 [81920, 1280], P('req', 'tp'), may hold values from -70 to 70
- dec_values: bfloat16 [81920, 1280], P('req', 'tp'), may hold values from -6 to 6
- dec_lens: int32 [512], replicated, may hold values from 1 to 41600, as said below
Outputs:
- pre_out: bfloat16 [65536, 1280], P('req', 'tp')
- dec_out: bfloat16 [512, 1280], P('req', 'tp')
Inputs may be any that keep to these rules, and one draw needn't show every extreme that they name: `pre_lens`: at least one prefill block has all 384 cached rows valid. `dec_lens`: the lengths sum to 61440; request 0 has exactly 41600 rows, every other request fewer.
All inputs are finite; a program needn't handle non-finite values.
Results may differ from a plain program's by a relative error of at most 0.012.
The roundings to bfloat16 on the way count: a program that leaves them out, or rounds other values in their place, can miss the bound.
Values may be sent and summed in bfloat16 or wider, within the bound.
No kernel may reach another device: no remote copies, remote signals or barrier semaphores. Data moves between devices by JAX's collectives and lax.ppermute only.
A program may use at most 64 MiB of HBM per device.

v0:
```python
import math
import jax
import jax.numpy as jnp
from jax import lax
from jax.sharding import PartitionSpec as P

HD = 80
EPSILON = 1e-06
MASKED_SCORE = -1e30


def normalize(tokens, norm_gain):
    tokens_f = tokens.astype(jnp.float32)
    mean_square = jnp.mean(tokens_f * tokens_f, axis=-1, keepdims=True)
    return (tokens_f * lax.rsqrt(mean_square + EPSILON) * norm_gain).astype(jnp.bfloat16)


def project(hidden, w_qkv):
    return tuple(
        (
            jnp.dot(hidden, w_qkv[matrix_index], preferred_element_type=jnp.float32).astype(
                jnp.bfloat16
            )
            for matrix_index in range(3)
        )
    )


def rounded(weights):
    held = lax.optimization_barrier(weights.astype(jnp.bfloat16))
    return held.astype(jnp.float32)


def prefill_attention(
    query_pre, key_pre, value_pre, pre_keys, pre_values, prefix, local_heads, score_scale
):
    rows_pre = query_pre.shape[0]
    cached = pre_keys.shape[0]
    keys_all = jnp.concatenate([pre_keys, key_pre], axis=0).reshape(-1, local_heads, HD)
    values_all = jnp.concatenate([pre_values, value_pre], axis=0).reshape(-1, local_heads, HD)
    scores = (
        jnp.einsum(
            "phd,rhd->hpr",
            query_pre.reshape(rows_pre, local_heads, HD),
            keys_all,
            preferred_element_type=jnp.float32,
        )
        * score_scale
    )
    column = jnp.arange(keys_all.shape[0], dtype=jnp.int32)[None, :]
    position = jnp.arange(rows_pre, dtype=jnp.int32)[:, None]
    allowed = jnp.where(column < cached, column < prefix, column - cached <= position)
    scores = jnp.where(allowed[None], scores, MASKED_SCORE)
    row_top = jnp.max(scores, axis=-1, keepdims=True)
    weights = jnp.where(allowed[None], jnp.exp(scores - row_top), 0.0)
    totals = jnp.transpose(jnp.sum(weights, axis=-1))
    mixed = (
        jnp.einsum(
            "hpr,rhd->phd",
            weights.astype(jnp.bfloat16),
            values_all,
            preferred_element_type=jnp.float32,
        )
        / totals[..., None]
    )
    return mixed.reshape(rows_pre, local_heads * HD).astype(jnp.bfloat16)


def body(
    x_pre,
    x_dec,
    norm_gain,
    w_qkv,
    w_out,
    pre_keys,
    pre_values,
    pre_lens,
    dec_keys,
    dec_values,
    dec_lens,
):
    full_pre, full_dec = (
        lax.all_gather(x_pre, "tp", axis=1, tiled=True),
        lax.all_gather(x_dec, "tp", axis=1, tiled=True),
    )
    local_width = w_qkv.shape[2]
    local_heads = local_width // HD
    score_scale = 1.0 / math.sqrt(HD)
    query_pre, key_pre, value_pre = project(normalize(full_pre, norm_gain), w_qkv)
    query_dec, key_dec, value_dec = project(normalize(full_dec, norm_gain), w_qkv)
    attn_pre = prefill_attention(
        query_pre, key_pre, value_pre, pre_keys, pre_values, pre_lens[0], local_heads, score_scale
    )
    all_queries = lax.all_gather(query_dec, "req", axis=0, tiled=True)
    requests = all_queries.shape[0]
    own_rows = query_dec.shape[0]
    pool_rows = dec_keys.shape[0]
    device = lax.axis_index("req")
    starts = jnp.cumsum(dec_lens) - dec_lens
    global_rows = device * pool_rows + jnp.arange(pool_rows, dtype=jnp.int32)
    allowed = (global_rows[None, :] >= starts[:, None]) & (
        global_rows[None, :] < (starts + dec_lens)[:, None]
    )
    cache_scores = (
        jnp.einsum(
            "qhd,rhd->qhr",
            all_queries.reshape(requests, local_heads, HD),
            dec_keys.reshape(pool_rows, local_heads, HD),
            preferred_element_type=jnp.float32,
        )
        * score_scale
    )
    cache_scores = jnp.where(allowed[:, None, :], cache_scores, MASKED_SCORE)
    self_score = (
        jnp.sum(
            query_dec.astype(jnp.float32).reshape(own_rows, local_heads, HD)
            * key_dec.astype(jnp.float32).reshape(own_rows, local_heads, HD),
            axis=-1,
        )
        * score_scale
    )
    self_rows = lax.dynamic_update_slice_in_dim(
        jnp.full((requests, local_heads), MASKED_SCORE, jnp.float32),
        self_score,
        device * own_rows,
        0,
    )
    local_top = jnp.maximum(jnp.max(cache_scores, axis=-1), self_rows)
    row_top = lax.pmax(local_top, "req")
    weights = jnp.where(allowed[:, None, :], jnp.exp(cache_scores - row_top[..., None]), 0.0)
    totals = jnp.sum(weights, axis=-1)
    partial_value = jnp.einsum(
        "qhr,rhd->qhd",
        weights.astype(jnp.bfloat16),
        dec_values.reshape(pool_rows, local_heads, HD),
        preferred_element_type=jnp.float32,
    ).reshape(requests, local_width)
    totals_all, partial_all = lax.psum((totals, partial_value), "req")
    own_totals = lax.dynamic_slice_in_dim(totals_all, device * own_rows, own_rows, 0)
    own_partial = lax.dynamic_slice_in_dim(partial_all, device * own_rows, own_rows, 0)
    own_top = lax.dynamic_slice_in_dim(row_top, device * own_rows, own_rows, 0)
    self_weight = jnp.exp(self_score - own_top)
    numerator = own_partial.reshape(own_rows, local_heads, HD) + rounded(self_weight)[
        ..., None
    ] * value_dec.astype(jnp.float32).reshape(own_rows, local_heads, HD)
    denominator = own_totals + self_weight
    attn_dec = (
        (numerator / denominator[..., None]).reshape(own_rows, local_width).astype(jnp.bfloat16)
    )
    terms_pre = jnp.dot(attn_pre, w_out, preferred_element_type=jnp.float32)
    terms_dec = jnp.dot(attn_dec, w_out, preferred_element_type=jnp.float32)
    out_pre, out_dec = (
        lax.psum_scatter(terms_pre, "tp", scatter_dimension=1, tiled=True),
        lax.psum_scatter(terms_dec, "tp", scatter_dimension=1, tiled=True),
    )
    return (out_pre.astype(jnp.bfloat16), out_dec.astype(jnp.bfloat16))


def solution(mesh):
    return jax.shard_map(
        body,
        mesh=mesh,
        in_specs=(
            P("req", "tp"),
            P("req", "tp"),
            P(),
            P(None, None, "tp"),
            P("tp", None),
            P("req", "tp"),
            P("req", "tp"),
            P("req"),
            P("req", "tp"),
            P("req", "tp"),
            P(),
        ),
        out_specs=(P("req", "tp"), P("req", "tp")),
        check_vma=False,
    )
```

profile of v0, /device:TPU:1, one launch (start us, length us, event | category | flops | bytes accessed | tf_op | source)
XLA Modules:
  0.0 785.2 jit_solution(5157148201678637434)
XLA Ops:
  8.1 10.6 %all-gather = bf16[4,320,4]{1,2,0:T(4,128)(2,1)S(1)} all-gather(bf16[1,320,4]{1,2,0:T(4,128)(2,1)} %bitcast.80), channel_id=1, replica_groups=mesh['req'=128,'tp'=4] {'tp'}, dimensions={0}, use_global_device_ids=true | all-gather | bytes 12800 | tf_op jit(solution)/shard_map/all_gather | solution.py:84
  19.7 1.4 convolution_convert_fusion.5
  21.1 1.5 fusion.36
  22.9 1.0 reduce-window.9
  24.9 92.8 %all-gather.1 = bf16[128,4,320]{2,1,0:T(4,128)(2,1)S(1)} all-gather(bf16[1,4,320]{2,1,0:T(4,128)(2,1)S(1)} %bitcast.78), channel_id=1, replica_groups=mesh['req'=128,'tp'=4] {'req'}, dimensions={0}, use_global_device_ids=true | all-gather | bytes 330240 | tf_op jit(solution)/shard_map/all_gather | solution.py:94
  118.7 3.6 bitcast_reduce_fusion
  122.3 250.3 %pmax.7 = f32[512,4]{0,1:T(4,128)S(1)} all-reduce(f32[512,4]{0,1:T(4,128)S(1)} %max.5), channel_id=1, replica_groups=mesh['req'=128,'tp'=4] {'req'}, use_global_device_ids=true, to_apply=%region_9.10 | all-reduce | flops 2048 | bytes 16384 | tf_op jit(solution)/shard_map/pmax | solution.py:129
  372.6 3.6 fusion.16
  376.2 1.1 copy.23
  378.0 3.8 fusion.6
  381.9 253.8 %psum.15 = f32[512,4]{0,1:T(4,128)S(1)} all-reduce(f32[512,4]{0,1:T(4,128)S(1)} %fusion.6), channel_id=1, replica_groups=mesh['req'=128,'tp'=4] {'req'}, use_global_device_ids=true, to_apply=%region_12.13 | all-reduce | flops 2048 | bytes 16384 | tf_op jit(solution)/shard_map/psum | solution.py:138
  636.9 1.1 fusion.20
  638.1 63.4 %all-reduce.2.cloned.1.call-done = f32[512,320]{1,0:T(8,128)} async-done(((f32[512,320]{1,0:T(8,128)}), f32[512,320]{1,0:T(8,128)}) %all-reduce.2.cloned.1.call-update) | async-done | bytes 655376 | tf_op jit(solution)/shard_map/psum | solution.py:138
  701.5 2.9 convolution_bitcast_fusion
  704.7 1.7 fusion.13
  706.4 2.1 convolution_convert_fusion
  710.9 1.4 convolution_convert_fusion.1
  712.4 6.7 fusion.65
  719.1 3.3 fusion.27
  722.4 2.4 fusion.66
  724.8 5.1 reduce-scatter.7.cloned.1.call-done
  729.9 1.6 copy.27
  731.5 44.2 %reduce-scatter.5.cloned.1.call-done = f32[512,320]{0,1:T(8,128)} async-done(((f32[512,1280]{0,1:T(8,128)}), f32[512,320]{0,1:T(8,128)}) %reduce-scatter.5.cloned.1.call-update) | async-done | bytes 655376 | tf_op jit(solution)/shard_map/reduce_scatter | solution.py:153
  775.7 1.9 convert_element_type.74
  (59 shorter events, 7.3 us)
Async XLA Ops:
  8.0 693.5 %copy-start = (bf16[320,1280]{1,0:T(8,128)(2,1)S(1)}, bf16[320,1280]{1,0:T(8,128)(2,1)}, u32[]{:S(2)}) copy-start(bf16[320,1280]{1,0:T(8,128)(2,1)} %param.15) | copy-start | bytes 2457604
  8.0 110.7 %copy-start.7 = (bf16[640,320]{0,1:T(8,128)(2,1)S(1)}, bf16[640,320]{0,1:T(8,128)(2,1)}, u32[]{:S(2)}) copy-start(bf16[640,320]{0,1:T(8,128)(2,1)} %param.19) | copy-start | bytes 1228804
  8.0 693.5 %all-reduce.2.cloned.1.call-start = ((), (), s32[]{:S(2)}) async-start(), calls=%async_computation.4 | async-start | bytes 1572864 | tf_op jit(solution)/shard_map/psum | solution.py:138
  118.7 253.9 %copy-start.8 = (bf16[640,320]{0,1:T(8,128)(2,1)S(1)}, bf16[640,320]{0,1:T(8,128)(2,1)}, u32[]{:S(2)}) copy-start(bf16[640,320]{0,1:T(8,128)(2,1)} %param.20) | copy-start | bytes 1228804
  377.4 327.3 %all-gather.4.cloned.1.call-start = ((), (), s32[]{:S(2)}) async-start(), calls=%async_computation.2 | async-start | bytes 1638400 | tf_op jit(solution)/shard_map/all_gather | solution.py:83
  378.0 351.9 %reduce-scatter.7.cloned.1.call-start = ((), (), s32[]{:S(2)}) async-start(), calls=%async_computation.5 | async-start | bytes 819200
  381.8 324.6 %copy-start.1 = (bf16[3,1280,320]{1,2,0:T(8,128)(2,1)S(1)}, bf16[3,1280,320]{1,2,0:T(8,128)(2,1)}, u32[]{:S(2)}) copy-start(bf16[3,1280,320]{1,2,0:T(8,128)(2,1)} %param.14) | copy-start | bytes 7372804
  381.8 324.5 %copy-start.6 = (f32[1280]{0:T(1024)S(1)}, f32[1280]{0:T(1024)}, u32[]{:S(2)}) copy-start(f32[1280]{0:T(1024)} %param.13) | copy-start | bytes 15364
  704.5 4.1 copy-start.4
  704.5 71.2 %reduce-scatter.5.cloned.1.call-start = ((), (), s32[]{:S(2)}) async-start(), calls=%async_computation.3 | async-start | bytes 3276800 | tf_op jit(solution)/shard_map/reduce_scatter | solution.py:153
  706.4 3.0 copy-start.2
  708.5 1.6 copy-start.5
  712.4 6.7 copy-start.3
Sparse Core Ops, SparseCore 0:
  377.5 323.8 all-reduce.1
Sparse Core Ops, SparseCore 1:
  380.0 21.8 all-gather.3
  704.5 25.3 reduce-scatter.6
  732.6 43.1 reduce-scatter.4
where the time goes:
time: 786 us; the launch traced here: 785 us
  blocking collectives  607 us (77%)
  waiting for transfers between devices  113 us (14%)
  matrix products  29.6 us (4%)
  between operations  16.5 us (2%)
  other arithmetic  13.4 us (2%)
    psum x1, blocking collectives, body(): totals_all, partial_all = lax.psum((totals, partial_value), 'req')  254 us
    pmax x1, blocking collectives, body(): row_top = lax.pmax(local_top, 'req')  250 us
    all_gather x1, blocking collectives, body(): all_queries = lax.all_gather(query_dec, 'req', axis=0, tiled=True)  92.8 us
    psum x1, waiting for transfers between devices, body(): totals_all, partial_all = lax.psum((totals, partial_value), 'req')  63.4 us
    reduce_scatter x1, waiting for transfers between devices, body(): lax.psum_scatter(terms_pre, 'tp', scatter_dimension=1, tiled=True)  44.2 us
  transfers between devices with their start and end apart: 4, of which 3 were waited for; matrix products, arithmetic and copies ran while one was open for 4% of the time, Pallas kernels for 0%

commit v1 on v0

--- a/solution.py
+++ b/solution.py
@@ -91,7 +91,9 @@
     attn_pre = prefill_attention(
         query_pre, key_pre, value_pre, pre_keys, pre_values, pre_lens[0], local_heads, score_scale
     )
-    all_queries = lax.all_gather(query_dec, "req", axis=0, tiled=True)
+    all_queries = jnp.concatenate(
+        lax.all_to_all(jnp.stack([query_dec] * lax.axis_size("req")), "req", 0, 0), axis=0
+    )
     requests = all_queries.shape[0]
     own_rows = query_dec.shape[0]
     pool_rows = dec_keys.shape[0]

time: 786 us -> 739 us (0.940)
  blocking collectives: 607 us -> 514 us
  waiting for transfers between devices: 113 us -> 138 us
  starting transfers between devices: 0.35 us -> 22.8 us
    all_gather x1 -> x0, blocking collectives: 92.8 us -> none  [body(): all_queries = lax.all_gather(query_dec, 'req', axis=0, tiled=True)]
    all_to_all x0 -> x1, waiting for transfers between devices: none -> 24.8 us  [body(): lax.all_to_all(jnp.stack([query_dec] * lax.axis_size('req')), 'req', 0, 0)]
    all_to_all x0 -> x1, starting transfers between devices: none -> 22.5 us  [body(): lax.all_to_all(jnp.stack([query_dec] * lax.axis_size('req')), 'req', 0, 0)]
  transfers between devices with their start and end apart: 4 -> 5, of which waited for: 3 -> 4; matrix products, arithmetic and copies ran while one was open for 4% -> 4% of each run, Pallas kernels for 0% -> 0%
where the time goes in v1:
time: 739 us
  blocking collectives  514 us (70%)
  waiting for transfers between devices  138 us (19%)
  matrix products  29.6 us (4%)
  starting transfers between devices  22.8 us (3%)
  between operations  16.5 us (2%)
  other arithmetic  12.1 us (2%)
    pmax x1, blocking collectives, body(): row_top = lax.pmax(local_top, 'req')  252 us
    psum x1, blocking collectives, body(): totals_all, partial_all = lax.psum((totals, partial_value), 'req')  251 us
    psum x1, waiting for transfers between devices, body(): totals_all, partial_all = lax.psum((totals, partial_value), 'req')  63.5 us
    reduce_scatter x1, waiting for transfers between devices, body(): lax.psum_scatter(terms_pre, 'tp', scatter_dimension=1, tiled=True)  44.2 us
    all_to_all x1, waiting for transfers between devices, body(): lax.all_to_all(jnp.stack([query_dec] * lax.axis_size('req')), 'req', 0, 0)  24.8 us
    all_to_all x1, starting transfers between devices, body(): lax.all_to_all(jnp.stack([query_dec] * lax.axis_size('req')), 'req', 0, 0)  22.5 us
  transfers between devices with their start and end apart: 5, of which 4 were waited for; matrix products, arithmetic and copies ran while one was open for 4% of the time, Pallas kernels for 0%

profile of v1, /device:TPU:1, one launch (start us, length us, event | category | flops | bytes accessed | tf_op | source)
XLA Modules:
  0.0 738.6 jit_solution(16928343992734676572)
XLA Ops:
  8.0 10.6 %all-gather = bf16[4,320,4]{1,2,0:T(4,128)(2,1)S(1)} all-gather(bf16[1,320,4]{1,2,0:T(4,128)(2,1)} %bitcast.78), channel_id=1, replica_groups=mesh['req'=128,'tp'=4] {'tp'}, dimensions={0}, use_global_device_ids=true | all-gather | bytes 12800 | tf_op jit(solution)/shard_map/all_gather | solution.py:84
  19.6 1.4 convolution_convert_fusion.5
  21.9 22.5 %all-to-all-start = ((bf16[128,4,320]{2,1,0:T(4,128)(2,1)}), bf16[128,4,320]{2,1,0:T(4,128)(2,1)S(1)}, u32[]{:S(2)}, u32[]{:S(2)}) async-start(bf16[128,4,320]{2,1,0:T(4,128)(2,1)} %stack.2), calls=%async_computation.1 | async-start | bytes 786432 | tf_op jit(solution)/shard_map/all_to_all | solution.py:95
  44.5 1.4 fusion.36
  47.5 24.8 %all-to-all-done = bf16[128,4,320]{2,1,0:T(4,128)(2,1)S(1)} async-done(((bf16[128,4,320]{2,1,0:T(4,128)(2,1)}), bf16[128,4,320]{2,1,0:T(4,128)(2,1)S(1)}, u32[]{:S(2)}, u32[]{:S(2)}) %all-to-all-start) | async-done | bytes 327712 | tf_op jit(solution)/shard_map/all_to_all | solution.py:95
  72.7 3.6 bitcast_reduce_fusion
  76.3 252.2 %pmax.7 = f32[512,4]{0,1:T(4,128)S(1)} all-reduce(f32[512,4]{0,1:T(4,128)S(1)} %max.5), channel_id=1, replica_groups=mesh['req'=128,'tp'=4] {'req'}, use_global_device_ids=true, to_apply=%region_9.10 | all-reduce | flops 2048 | bytes 16384 | tf_op jit(solution)/shard_map/pmax | solution.py:131
  328.5 3.6 fusion.16
  332.2 1.1 copy.23
  334.6 1.1 fusion.20
  335.8 3.8 fusion.6
  339.6 251.2 %psum.15 = f32[512,4]{0,1:T(4,128)S(1)} all-reduce(f32[512,4]{0,1:T(4,128)S(1)} %fusion.6), channel_id=1, replica_groups=mesh['req'=128,'tp'=4] {'req'}, use_global_device_ids=true, to_apply=%region_12.13 | all-reduce | flops 2048 | bytes 16384 | tf_op jit(solution)/shard_map/psum | solution.py:140
  591.4 63.5 %all-reduce.2.cloned.1.call-done = f32[512,320]{1,0:T(8,128)} async-done(((f32[512,320]{1,0:T(8,128)}), f32[512,320]{1,0:T(8,128)}) %all-reduce.2.cloned.1.call-update) | async-done | bytes 655376 | tf_op jit(solution)/shard_map/psum | solution.py:140
  654.9 2.9 convolution_bitcast_fusion
  658.1 1.7 fusion.13
  659.8 2.1 convolution_convert_fusion
  664.4 1.4 convolution_convert_fusion.1
  665.8 6.7 fusion.65
  672.5 3.3 fusion.27
  675.8 2.4 fusion.66
  678.2 5.1 reduce-scatter.7.cloned.1.call-done
  683.3 1.6 copy.27
  684.9 44.2 %reduce-scatter.5.cloned.1.call-done = f32[512,320]{0,1:T(8,128)} async-done(((f32[512,1280]{0,1:T(8,128)}), f32[512,320]{0,1:T(8,128)}) %reduce-scatter.5.cloned.1.call-update) | async-done | bytes 655376 | tf_op jit(solution)/shard_map/reduce_scatter | solution.py:155
  729.2 1.9 convert_element_type.74
  (63 shorter events, 7.8 us)
Async XLA Ops:
  8.0 646.9 %copy-start = (bf16[320,1280]{1,0:T(8,128)(2,1)S(1)}, bf16[320,1280]{1,0:T(8,128)(2,1)}, u32[]{:S(2)}) copy-start(bf16[320,1280]{1,0:T(8,128)(2,1)} %param.15) | copy-start | bytes 2457604
  8.0 38.2 %copy-start.7 = (s32[512]{0:T(512)S(1)}, s32[512]{0:T(512)}, u32[]{:S(2)}) copy-start(s32[512]{0:T(512)} %param.21) | copy-start | bytes 6148
  8.0 64.6 %copy-start.8 = (bf16[640,320]{0,1:T(8,128)(2,1)S(1)}, bf16[640,320]{0,1:T(8,128)(2,1)}, u32[]{:S(2)}) copy-start(bf16[640,320]{0,1:T(8,128)(2,1)} %param.19) | copy-start | bytes 1228804
  21.9 50.3 %all-to-all-start = ((bf16[128,4,320]{2,1,0:T(4,128)(2,1)}), bf16[128,4,320]{2,1,0:T(4,128)(2,1)S(1)}, u32[]{:S(2)}, u32[]{:S(2)}) async-start(bf16[128,4,320]{2,1,0:T(4,128)(2,1)} %stack.2), calls=%async_computation.1 | async-start | bytes 786432 | tf_op jit(solution)/shard_map/all_to_all | solution.py:95
  44.4 610.5 %all-reduce.2.cloned.1.call-start = ((), (), s32[]{:S(2)}) async-start(), calls=%async_computation.5 | async-start | bytes 1572864 | tf_op jit(solution)/shard_map/psum | solution.py:140
  72.7 255.8 %copy-start.9 = (bf16[640,320]{0,1:T(8,128)(2,1)S(1)}, bf16[640,320]{0,1:T(8,128)(2,1)}, u32[]{:S(2)}) copy-start(bf16[640,320]{0,1:T(8,128)(2,1)} %param.20) | copy-start | bytes 1228804
  333.3 324.8 %all-gather.3.cloned.1.call-start = ((), (), s32[]{:S(2)}) async-start(), calls=%async_computation.3 | async-start | bytes 1638400 | tf_op jit(solution)/shard_map/all_gather | solution.py:83
  333.9 349.4 %reduce-scatter.7.cloned.1.call-start = ((), (), s32[]{:S(2)}) async-start(), calls=%async_computation.6 | async-start | bytes 819200
  339.6 320.2 %copy-start.1 = (bf16[3,1280,320]{1,2,0:T(8,128)(2,1)S(1)}, bf16[3,1280,320]{1,2,0:T(8,128)(2,1)}, u32[]{:S(2)}) copy-start(bf16[3,1280,320]{1,2,0:T(8,128)(2,1)} %param.14) | copy-start | bytes 7372804
  339.6 320.2 %copy-start.6 = (f32[1280]{0:T(1024)S(1)}, f32[1280]{0:T(1024)}, u32[]{:S(2)}) copy-start(f32[1280]{0:T(1024)} %param.13) | copy-start | bytes 15364
  657.9 4.1 copy-start.4
  657.9 71.3 %reduce-scatter.5.cloned.1.call-start = ((), (), s32[]{:S(2)}) async-start(), calls=%async_computation.4 | async-start | bytes 3276800 | tf_op jit(solution)/shard_map/reduce_scatter | solution.py:155
  659.8 3.0 copy-start.2
  661.9 1.6 copy-start.5
  665.8 6.7 copy-start.3
Sparse Core Ops, SparseCore 0:
  333.5 321.4 all-reduce.1
Sparse Core Ops, SparseCore 1:
  335.9 19.2 all-gather.2
  658.0 25.3 reduce-scatter.6
  686.1 43.1 reduce-scatter.4
